TPU v7x, 32 devices: a whole 2x2x4 slice. The times are simulated.
32 devices in a mesh: tm: 4 (over x, core), rows: 8 (over z, y).
Axes of the slice: x: 2, y: 2, z: 4, core: 2. Of those that a mesh axis runs over, the one named last changes fastest.
Arguments:
- latent: bfloat16 [16, 192, 32, 128], P('tm', None, 'rows'), may hold values from -6 to 6
- clip_ids: int32 [16], replicated, may hold values from 0 to 1, as said below
- gain_in: float32 [192], replicated, may hold values from 0.1 to 1.9
- conv_in: bfloat16 [3, 3, 3, 96, 192], replicated, may hold values from -0.078125 to 0.078125
- bias_in: float32 [96], replicated, may hold values from -3 to 3
- gain_mid: float32 [96], replicated, may hold values from 0.1 to 1.9
- conv_mid: bfloat16 [3, 3, 3, 96, 96], replicated, may hold values from -0.125 to 0.125
- bias_mid: float32 [96], replicated, may hold values from -3 to 3
- skip_weight: bfloat16 [96, 192], replicated, may hold values from -0.4375 to 0.4375
- skip_bias: float32 [96], replicated, may hold values from -3 to 3
Outputs:
- decoded: bfloat16 [16, 96, 32, 128], P('tm', None, 'rows')
Inputs may be any that keep to these rules, and one draw needn't show every extreme that they name: `clip_ids`: clip number of each frame; numbers never fall along the frames and every number appears; each clip lies on consecutive frames, and every clip other than the window's first and last holds 1 + 4 k frames, at most 21.
All inputs are finite; a program needn't handle non-finite values.
Results may differ from a plain program's by a relative error of at most 0.0075.
Values may be sent and summed in bfloat16 or wider, within the bound.
No kernel may reach another device: no remote copies, remote signals or barrier semaphores. Data moves between devices by JAX's collectives and lax.ppermute only.
A program may use at most 64 MiB of HBM per device.

v0:
```python
import jax
import jax.numpy as jnp
from jax import lax
from jax.experimental import pallas as pl
from jax.experimental.pallas import tpu as pltpu
from jax.sharding import PartitionSpec as P


F32 = jnp.float32
BF16 = jnp.bfloat16
VMEM = pl.BlockSpec(memory_space=pltpu.VMEM)
HBM = pl.BlockSpec(memory_space=pltpu.HBM)


def silu_norm(values, gain):
    mean_sq = jnp.mean(values * values, axis=0, keepdims=True)
    scaled = values * lax.rsqrt(mean_sq + 1e-06) * gain
    return scaled / (1.0 + jnp.exp(-scaled))


def column_taps(act):
    lane = lax.broadcasted_iota(jnp.int32, act.shape, 1)
    width = act.shape[1]
    left = jnp.where(lane == 0, 0.0, pltpu.roll(act, 1, 1))
    right = jnp.where(lane == width - 1, 0.0, pltpu.roll(act, width - 1, 1))
    return left.astype(BF16), act.astype(BF16), right.astype(BF16)


def spread(vector, width):
    return jnp.broadcast_to(vector, (width, vector.shape[1])).T


def kept(clip_ref, frame, back):
    final = clip_ref.shape[0] - 1
    here = clip_ref[jnp.clip(frame, 0, final)]
    there = clip_ref[jnp.clip(frame - back, 0, final)]
    return (frame - back >= 0) & (here == there)


def fold_taps(weight_ref, row_tap, taps):
    return jnp.concatenate([weight_ref[t, row_tap, j] for t in taps for j in range(3)], axis=1)


def dot(a, b):
    return jnp.dot(a, b, preferred_element_type=F32)


def norm_frame(lat_ref, frame, rows, gain, xs_ref):
    _, chans, height, width = lat_ref.shape
    values = lat_ref[frame].reshape(chans, height * width)
    for n, r in enumerate(rows):
        act = silu_norm(values[:, r * width : (r + 1) * width].astype(F32), gain)
        for j, tap in enumerate(column_taps(act)):
            xs_ref[pl.ds((frame * 3 + j) * chans, chans), n * width : (n + 1) * width] = tap


def conv_frame(xs_ref, wt_ref, keep_ref, out, lag):
    depth = wt_ref.shape[1] // 3
    columns = xs_ref.shape[1]
    taps = [t for t in range(3) if 0 <= out - 2 + t + lag < xs_ref.shape[0] // depth]
    blocks = []
    for t in taps:
        block = xs_ref[pl.ds((out - 2 + t + lag) * depth, depth), :]
        if t < 2:
            keep = keep_ref[2 * out + 1 - t]
            high, width = keep.shape
            keep = jnp.concatenate([keep] * (columns // width), axis=1)
            block = (block.reshape(depth // high, high, columns) * keep[None]).reshape(depth, columns)
        blocks.append(block)
    first = taps[0] * depth
    spare = first % 128
    if spare:
        blocks.insert(0, jnp.zeros((spare, columns), BF16))
    weight = wt_ref[:, first - spare : (taps[-1] + 1) * depth]
    outs = weight.shape[0] // 3
    y = dot(weight, blocks[0] if len(blocks) == 1 else jnp.concatenate(blocks, axis=0))
    return [y[i * outs : (i + 1) * outs] for i in range(3)]


def first_kernel(clip_hbm, lat_hbm, weight_hbm, gain_hbm, wt_ref, up_ref, cross_ref, edge_ref, lat_ref, keep_ref, xs_ref, weight_ref, gain_ref, clip_ref, sems):
    frames, _, height, width = lat_ref.shape
    outs = weight_ref.shape[3]
    start = lax.axis_index("tm") * frames
    pairs = [(gain_hbm, gain_ref)] + [(lat_hbm.at[f], lat_ref.at[f]) for f in range(frames)] + [(clip_hbm, clip_ref)]
    pairs += [(weight_hbm, weight_ref)]
    copies = [pltpu.make_async_copy(a, b, sems.at[n]) for n, (a, b) in enumerate(pairs)]
    for copy in copies:
        copy.start()
    copies[0].wait()
    gain = spread(gain_ref[...], width)
    for f in range(frames):
        copies[1 + f].wait()
        norm_frame(lat_ref, f, (height - 2, height - 1), gain, xs_ref)
    copies[1 + frames].wait()
    for out in range(frames + 2):
        for back in (1, 2):
            flag = jnp.where(kept(clip_ref, start + out, back), 1.0, 0.0)
            keep_ref[2 * out + back - 1] = jnp.full(keep_ref.shape[1:], flag, F32).astype(BF16)

    def message(out):
        y0, y1, y2 = conv_frame(xs_ref, wt_ref, keep_ref, out, 0)
        far = y0[:, :width] + y1[:, width:]
        for ref, place in ((up_ref, out), (cross_ref, out - frames + 2)):
            if 0 <= place < ref.shape[0]:
                ref[place, :, :width] = far.astype(BF16)
                ref[place, :, width:] = y0[:, width:].astype(BF16)
        edge_ref[out, :, :width] = y2[:, :width]
        edge_ref[out, :, width : 2 * width] = y1[:, :width] + y2[:, width:]
        edge_ref[out, :, 2 * width :] = far

    for copy in copies[2 + frames :]:
        copy.wait()
    for i in range(3):
        wt_ref[i * outs : (i + 1) * outs, :] = fold_taps(weight_ref, i, range(3))
    for out in range(frames + 2):
        message(out)


def inner_rows(xs_ref, wt_ref, keep_ref, edge_ref, out, width):
    inner = xs_ref.shape[1] // width
    y0, y1, y2 = conv_frame(xs_ref, wt_ref, keep_ref, out, 0)
    rows = []
    for h in range(-1, inner + 2):
        total = None
        for tap, row in ((y0, h - 1), (y1, h), (y2, h + 1)):
            if 0 <= row < inner:
                term = tap[:, row * width : (row + 1) * width]
                total = term if total is None else total + term
        if h >= inner - 1:
            e = h - inner + 1
            term = edge_ref[out, :, e * width : (e + 1) * width]
            total = term if total is None else total + term
        rows.append(total)
    return rows


def inner_kernel(keep_ref, lat_ref, gain_ref, wt_ref, edge_ref, bias_ref, gain_mid_ref, part_ref, near_ref, early_ref, xs_ref, mid_ref):
    frames, _, height, width = lat_ref.shape
    gain = spread(gain_ref[...], width)
    bias, gain_mid = spread(bias_ref[...], width), spread(gain_mid_ref[...], width)
    mid_ref[0] = bias
    mid_ref[1] = gain_mid
    for f in range(frames):
        norm_frame(lat_ref, f, range(height - 2), gain, xs_ref)
    for k in range(4):
        rows = inner_rows(xs_ref, wt_ref, keep_ref, edge_ref, frames - 2 + k, width)
        for h, total in enumerate(rows, -1):
            if h < 1:
                cols = pl.ds((h + 1) * width, width)
                near_ref[k, :, cols] = total.astype(BF16)
                if k < 2:
                    part_ref[k, :, cols] = total
            else:
                if k < 2:
                    total = act_rows(total, h, height, bias, gain_mid)
                early_ref[k, :, (h - 1) * width : h * width] = total.astype(BF16)


def head_kernel(keep_ref, xs_ref, wt_ref, edge_ref, weight_ref, head_ref, w_ref):
    frames, outs, _ = head_ref.shape
    width = edge_ref.shape[2] // 3
    for i in range(3):
        w_ref[i * outs : (i + 1) * outs, :] = fold_taps(weight_ref, i, range(3))
    for out in range(frames):
        rows = inner_rows(xs_ref, wt_ref, keep_ref, edge_ref, out, width)
        for n, total in enumerate(rows):
            head_ref[out, :, n * width : (n + 1) * width] = total


def act_rows(total, h, height, bias, gain):
    hidden = (total + bias).astype(BF16).astype(F32)
    act = silu_norm(hidden, gain)
    if h == -1:
        return jnp.where(lax.axis_index("rows") > 0, act, 0.0)
    if h == height - 1:
        return jnp.where(lax.axis_index("rows") == lax.axis_size("rows") - 1, act, 0.0)
    return act


def act_taps(act_of, rows, frames, xs_ref, width):
    outs = xs_ref.shape[0] // (3 * (frames + 2))
    for s in range(-2, frames):
        for n, h in enumerate(rows):
            for j, tap in enumerate(column_taps(act_of(s, h))):
                xs_ref[pl.ds(((s + 2) * 3 + j) * outs, outs), n * width : (n + 1) * width] = tap


def edge_kernel(keep_ref, head_ref, part_ref, got_ref, before_ref, cross_ref, mid_ref, w_ref, down_ref, edge_ref, xs_ref):
    width = got_ref.shape[2] // 2
    frames = got_ref.shape[0]
    bias, gain = mid_ref[0], mid_ref[1]

    def act_of(s, h):
        cols = pl.ds((h + 1) * width, width)
        total = None
        if s >= 0:
            own = part_ref[s - frames + 2, :, cols] if s >= frames - 2 else head_ref[s, :, cols]
            total = own + got_ref[s, :, cols].astype(F32)
        if s < 2:
            sent = before_ref[s + 2, :, cols].astype(F32) + cross_ref[s + 2, :, cols].astype(F32)
            total = sent if total is None else total + sent
        return act_rows(total, h, 0, bias, gain)

    act_taps(act_of, (-1, 0), frames, xs_ref, width)
    for out in range(frames):
        y0, y1, y2 = conv_frame(xs_ref, w_ref, keep_ref, out, 2)
        down_ref[out, :, :width] = y2[:, :width].astype(BF16)
        down_ref[out, :, width:] = (y1[:, :width] + y2[:, width:]).astype(BF16)
        edge_ref[out, :, :width] = y0[:, :width] + y1[:, width:]
        edge_ref[out, :, width:] = y0[:, width:]


def body_kernel(keep_ref, head_ref, mine_ref, before_ref, w_ref, edge_ref, mid_ref, lat_ref, skip_ref, bias_mid_ref, skip_bias_ref, total_ref, xs_ref):
    frames, chans, height, width = lat_ref.shape
    bias, gain = mid_ref[0], mid_ref[1]
    shift = spread(bias_mid_ref[...] + skip_bias_ref[...], width)

    def act_of(s, h):
        cols = pl.ds((h - 1) * width, width)
        if s < 0:
            return before_ref[s + 2, :, cols].astype(F32)
        if s >= frames - 2:
            return mine_ref[s - frames + 2, :, cols].astype(F32)
        total = head_ref[s, :, (h + 1) * width : (h + 2) * width]
        if s < 2:
            total = total + before_ref[s + 2, :, cols].astype(F32)
        return act_rows(total, h, height, bias, gain)

    act_taps(act_of, range(1, height), frames, xs_ref, width)
    skip = skip_ref[...]
    for out in range(frames):
        y0, y1, y2 = conv_frame(xs_ref, w_ref, keep_ref, out, 2)
        short = dot(skip, lat_ref[out].reshape(chans, height * width))
        for r in range(height):
            cols = pl.ds(r * width, width)
            total = short[:, r * width : (r + 1) * width] + shift
            for tap, row in ((y0, r - 1), (y1, r), (y2, r + 1)):
                if 1 <= row < height:
                    total = total + tap[:, (row - 1) * width : row * width]
            if r < 2:
                total = total + edge_ref[out, :, cols]
            total_ref[out, :, cols] = total


def last_kernel(total_ref, below_ref, out_ref):
    frames, outs, height, width = out_ref.shape
    for f in range(frames):
        rows = [total_ref[f, :, r * width : (r + 1) * width] for r in range(height)]
        for n in range(2):
            rows[height - 2 + n] = rows[height - 2 + n] + below_ref[f, :, n * width : (n + 1) * width].astype(F32)
        out_ref[f] = jnp.concatenate(rows, axis=1).reshape(outs, height, width).astype(BF16)


def call(kernel, shapes, operands, flops, places=(), scratch=()):
    moved = sum(x.size * x.dtype.itemsize for x in operands) + sum(s.size * s.dtype.itemsize for s in shapes)
    single = len(shapes) == 1
    places = list(places) + [VMEM] * (len(operands) - len(places))
    return pl.pallas_call(
        kernel,
        out_shape=shapes[0] if single else tuple(shapes),
        in_specs=places,
        out_specs=VMEM if single else tuple(VMEM for _ in shapes),
        scratch_shapes=list(scratch),
        cost_estimate=pl.CostEstimate(flops=flops, bytes_accessed=moved, transcendentals=0),
        compiler_params=pltpu.CompilerParams(vmem_limit_bytes=20 << 20),
    )(*operands)


def moved_by(block, axis, distance):
    devices = range(lax.axis_size(axis))
    return lax.ppermute(block, axis, [(i, i + distance) for i in devices if i + distance in devices])


def moved_across(block):
    steps, lines = lax.axis_size("tm"), lax.axis_size("rows")
    route = [(t * lines + i, (t + 1) * lines + i + 1) for t in range(steps - 1) for i in range(lines - 1)]
    return lax.ppermute(block, ("tm", "rows"), route)


def shards(latent, clip_ids, gain_in, conv_in, bias_in, gain_mid, conv_mid, bias_mid, skip_weight, skip_bias):
    frames, chans, height, width = latent.shape
    outs = conv_in.shape[3]
    shape = jax.ShapeDtypeStruct
    row = lambda v: v.reshape(1, -1)
    deep, deep_mid, tall = 3 * chans, 3 * outs, 3 * outs
    work = 2 * tall * 3 * deep * frames * width
    wt, up, cross, edge, lat, keep = call(
        first_kernel,
        [
            shape((tall, 3 * deep), BF16),
            shape((frames, outs, 2 * width), BF16),
            shape((4, outs, 2 * width), BF16),
            shape((frames + 2, outs, 3 * width), F32),
            shape(latent.shape, BF16),
            shape((2 * (frames + 2), 16, width), BF16),
        ],
        tuple(pltpu.with_memory_space_constraint(x, pltpu.HBM) for x in (clip_ids, latent, conv_in, row(gain_in))),
        work * 2,
        [HBM] * 4,
        [
            pltpu.VMEM((frames * deep, 2 * width), BF16),
            pltpu.VMEM(conv_in.shape, BF16),
            pltpu.VMEM((1, chans), F32),
            pltpu.SMEM(clip_ids.shape, jnp.int32),
            pltpu.SemaphoreType.DMA((frames + 3,)),
        ],
    )
    got = moved_by(up, "rows", 1)
    cross_got = moved_across(cross)
    part, near, early, xs, mid = call(
        inner_kernel,
        [
            shape((2, outs, 2 * width), F32),
            shape((4, outs, 2 * width), BF16),
            shape((4, outs, (height - 1) * width), BF16),
            shape((frames * deep, (height - 2) * width), BF16),
            shape((2, outs, width), F32),
        ],
        (keep, lat, row(gain_in), wt, edge, row(bias_in), row(gain_mid)),
        work * (height - 2),
    )
    before_near = moved_by(near, "tm", 1)
    before_early = moved_by(early, "tm", 1)
    head, w_mid = call(
        head_kernel,
        [shape((frames - 2, outs, (height + 1) * width), F32), shape((tall, 3 * deep_mid), BF16)],
        (keep, xs, wt, edge, conv_mid),
        work,
    )
    down, edge_mid = call(
        edge_kernel,
        [shape((frames, outs, 2 * width), BF16), shape((frames, outs, 2 * width), F32)],
        (keep, head, part, got, before_near, cross_got, mid, w_mid),
        work,
        scratch=[pltpu.VMEM(((frames + 2) * deep_mid, 2 * width), BF16)],
    )
    below = moved_by(down, "rows", -1)
    total = call(
        body_kernel,
        [shape((frames, outs, height * width), F32)],
        (keep, head, early, before_early, w_mid, edge_mid, mid, lat, skip_weight, row(bias_mid), row(skip_bias)),
        work * (height - 1) // 2,
        scratch=[pltpu.VMEM(((frames + 2) * deep_mid, (height - 1) * width), BF16)],
    )
    return call(last_kernel, [shape((frames, outs, height, width), BF16)], (total, below), 1000)


def solution(mesh):
    return jax.shard_map(
        shards,
        mesh=mesh,
        in_specs=(P("tm", None, "rows", None), P(), P(), P(), P(), P(), P(), P(), P(), P()),
        out_specs=P("tm", None, "rows", None),
        check_vma=False,
    )
```

profile of v0, /device:TPU:0, one launch (start us, length us, event | category | flops | bytes accessed | tf_op | source)
XLA Modules:
  0.0 30.2 jit_solution(2438945933177401699)
XLA Ops:
  0.0 0.0 copy-start.4
  0.0 0.0 copy-start.5
  0.0 0.0 copy-start.6
  0.0 3.7 %shard_map.100 = (bf16[288,1728]{1,0:T(8,128)(2,1)S(1)}, bf16[4,96,256]{2,1,0:T(8,128)(2,1)S(1)}, bf16[4,96,256]{2,1,0:T(8,128)(2,1)S(1)}, f32[6,96,384]{2,1,0:T...) custom-call(s32[16]{0:T(128)} %clip_hbm.1, bf16[4,192,4,128]{3,2,1,0:T(4,128)(2,1)} %lat_hbm.1, ...), custom_call_target="tpu_custom_call" | custom-call | flops 1019215872 | bytes 4891456 | tf_op jit(solution)/shard_map/pallas_call | solution.py:258
  3.7 4.9 %collective-permute-start.1 = (bf16[4,96,256]{2,1,0:T(8,128)(2,1)S(1)}, bf16[4,96,256]{2,1,0:T(8,128)(2,1)S(1)}, u32[]{:S(2)}, u32[]{:S(2)}) collective-permute-start(bf16[4,96,256]{2,1,0:T(8,128)(2,1)S(1)} %get-tuple-element.29), channel_id=1, source_target_pairs={{0,1},{1,2},{2,3},{3,4},{4,5},{5,6},{6,7},{8,9},{9,10},{10,11},{11... | collective-permute-start | bytes 589832 | tf_op jit(solution)/shard_map/ppermute | solution.py:271
  8.6 2.6 %collective-permute-start.3 = (bf16[4,96,256]{2,1,0:T(8,128)(2,1)S(1)}, bf16[4,96,256]{2,1,0:T(8,128)(2,1)S(1)}, u32[]{:S(2)}, u32[]{:S(2)}) collective-permute-start(bf16[4,96,256]{2,1,0:T(8,128)(2,1)S(1)} %get-tuple-element.31), channel_id=1, source_target_pairs={{0,9},{1,10},{2,11},{3,12},{4,13},{5,14},{6,15},{8,17},{9,18},{10,... | collective-permute-start | bytes 589832 | tf_op jit(solution)/shard_map/ppermute | solution.py:277
  11.2 0.0 copy-done.4
  11.2 0.0 copy-done.5
  11.2 0.0 copy-done.6
  11.2 0.0 copy-start
  11.2 1.8 %shard_map.101 = (f32[2,96,256]{2,1,0:T(8,128)S(1)}, bf16[4,96,256]{2,1,0:T(8,128)(2,1)S(1)}, bf16[4,96,384]{2,1,0:T(8,128)(2,1)S(1)}, bf16[2304,256]{1,0:T(8,128)(2,1)S(1)}, f32[2,96,128]{2,1,0:T(8,128)S(1)}) custom-call(bf16[12,16,128]{2,1,0:T(8,128)(2,1)S(1)} %get-tuple-element.20.keep_ref, bf16[4,192,4,128]{3,2,1,0:T(4,128)(2,1)S(1)} %get-tuple-element.21.lat_ref, ...), custom_call_target="tpu_custom_call" | custom-call | flops 1019215872 | bytes 4683264 | tf_op jit(solution)/shard_map/pallas_call | solution.py:258
  13.0 3.8 %collective-permute-start.2 = (bf16[4,96,256]{2,1,0:T(8,128)(2,1)S(1)}, bf16[4,96,256]{2,1,0:T(8,128)(2,1)S(1)}, u32[]{:S(2)}, u32[]{:S(2)}) collective-permute-start(bf16[4,96,256]{2,1,0:T(8,128)(2,1)S(1)} %get-tuple-element.30), channel_id=1, source_target_pairs={{0,8},{8,16},{16,24},{1,9},{9,17},{17,25},{2,10},{10,18},{18,26},{... | collective-permute-start | bytes 589832 | tf_op jit(solution)/shard_map/ppermute | solution.py:271
  16.8 1.9 %collective-permute-start = (bf16[4,96,384]{2,1,0:T(8,128)(2,1)S(1)}, bf16[4,96,384]{2,1,0:T(8,128)(2,1)S(1)}, u32[]{:S(2)}, u32[]{:S(2)}) collective-permute-start(bf16[4,96,384]{2,1,0:T(8,128)(2,1)S(1)} %get-tuple-element.26.mine_ref), channel_id=1, source_target_pairs={{0,8},{8,16},{16,24},{1,9},{9,17},{17,25},{2,10},{10,18},{18,26},{... | collective-permute-start | bytes 884744 | tf_op jit(solution)/shard_map/ppermute | solution.py:271
  18.8 0.0 copy-done
  18.8 0.5 %shard_map.102 = (f32[2,96,640]{2,1,0:T(8,128)S(1)}, bf16[288,864]{1,0:T(8,128)(2,1)S(1)}) custom-call(bf16[12,16,128]{2,1,0:T(8,128)(2,1)S(1)} %get-tuple-element.20.keep_ref, bf16[2304,256]{1,0:T(8,128)(2,1)S(1)} %get-tuple-element.24.xs_ref, bf16[288,1728]{1,0:T(8,128)(2,1)S(1)} %get-tuple-element.22.wt_ref, ...), custom_call_target="tpu_custom_call" | custom-call | flops 509607936 | bytes 4595712 | tf_op jit(solution)/shard_map/pallas_call | solution.py:258
  19.3 0.0 copy-start.1
  19.3 0.0 copy-start.2
  19.3 0.0 copy-start.3
  19.3 0.0 collective-permute-done.1.got_ref
  19.3 0.0 collective-permute-done.3.cross_ref
  19.3 0.0 collective-permute-done.2.before_ref
  19.3 1.1 %shard_map.103 = (bf16[4,96,256]{2,1,0:T(8,128)(2,1)S(1)}, f32[4,96,256]{2,1,0:T(8,128)S(1)}) custom-call(bf16[12,16,128]{2,1,0:T(8,128)(2,1)S(1)} %get-tuple-element.20.keep_ref, f32[2,96,640]{2,1,0:T(8,128)S(1)} %get-tuple-element.25.head_ref, f32[2,96,256]{2,1,0:T(8,128)S(1)} %get-tuple-element.28.part_ref, ...), custom_call_target="tpu_custom_call" | custom-call | flops 509607936 | bytes 2512896 | tf_op jit(solution)/shard_map/pallas_call | solution.py:258
  20.5 1.3 %collective-permute-start.4 = (bf16[4,96,256]{2,1,0:T(8,128)(2,1)S(1)}, bf16[4,96,256]{2,1,0:T(8,128)(2,1)S(1)}, u32[]{:S(2)}, u32[]{:S(2)}) collective-permute-start(bf16[4,96,256]{2,1,0:T(8,128)(2,1)S(1)} %get-tuple-element.34), channel_id=1, source_target_pairs={{1,0},{2,1},{3,2},{4,3},{5,4},{6,5},{7,6},{9,8},{10,9},{11,10},{12... | collective-permute-start | bytes 589832 | tf_op jit(solution)/shard_map/ppermute | solution.py:271
  21.8 0.0 collective-permute-done.before_ref
  21.8 0.0 copy-done.1
  21.8 0.0 copy-done.2
  21.8 0.0 copy-done.3
  21.8 1.7 %shard_map.104.total_ref = f32[4,96,512]{2,1,0:T(8,128)S(1)} custom-call(bf16[12,16,128]{2,1,0:T(8,128)(2,1)S(1)} %get-tuple-element.20.keep_ref, f32[2,96,640]{2,1,0:T(8,128)S(1)} %get-tuple-element.25.head_ref, bf16[4,96,384]{2,1,0:T(8,128)(2,1)S(1)} %get-tuple-element.26.mine_ref, bf16[4,96,384]{2,1,0:T(8,128)(2,1)S(1)} %collective-permute-done.before_ref, ...), custom_call_target="tpu_custom_call" | custom-call | flops 764411904 | bytes 3730176 | tf_op jit(solution)/shard_map/pallas_call | solution.py:258
  23.5 5.7 %collective-permute-done.4.below_ref = bf16[4,96,256]{2,1,0:T(8,128)(2,1)S(1)} collective-permute-done((bf16[4,96,256]{2,1,0:T(8,128)(2,1)S(1)}, bf16[4,96,256]{2,1,0:T(8,128)(2,1)S(1)}, u32[]{:S(2)}, u32[]{:S(2)}) %collective-permute-start.4) | collective-permute-done | bytes 196640 | tf_op jit(solution)/shard_map/ppermute | solution.py:271
  29.3 1.0 %shard_map.105 = bf16[4,96,4,128]{3,2,1,0:T(4,128)(2,1)} custom-call(f32[4,96,512]{2,1,0:T(8,128)S(1)} %shard_map.104.total_ref, bf16[4,96,256]{2,1,0:T(8,128)(2,1)S(1)} %collective-permute-done.4.below_ref), custom_call_target="tpu_custom_call" | custom-call | flops 1000 | bytes 1376256 | tf_op jit(solution)/shard_map/pallas_call | solution.py:258
Async XLA Ops:
  0.0 11.2 %copy-start.4 = (f32[192]{0:T(256)S(1)}, f32[192]{0:T(256)}, u32[]{:S(2)}) copy-start(f32[192]{0:T(256)} %param.12) | copy-start | bytes 2308
  0.0 11.2 %copy-start.5 = (f32[96]{0:T(128)S(1)}, f32[96]{0:T(128)}, u32[]{:S(2)}) copy-start(f32[96]{0:T(128)} %param.14) | copy-start | bytes 1156
  0.0 11.2 %copy-start.6 = (f32[96]{0:T(128)S(1)}, f32[96]{0:T(128)}, u32[]{:S(2)}) copy-start(f32[96]{0:T(128)} %param.15) | copy-start | bytes 1156
  3.7 15.6 %collective-permute-start.1 = (bf16[4,96,256]{2,1,0:T(8,128)(2,1)S(1)}, bf16[4,96,256]{2,1,0:T(8,128)(2,1)S(1)}, u32[]{:S(2)}, u32[]{:S(2)}) collective-permute-start(bf16[4,96,256]{2,1,0:T(8,128)(2,1)S(1)} %get-tuple-element.29), channel_id=1, source_target_pairs={{0,1},{1,2},{2,3},{3,4},{4,5},{5,6},{6,7},{8,9},{9,10},{10,11},{11... | collective-permute-start | bytes 589832 | tf_op jit(solution)/shard_map/ppermute | solution.py:271
  8.6 10.7 %collective-permute-start.3 = (bf16[4,96,256]{2,1,0:T(8,128)(2,1)S(1)}, bf16[4,96,256]{2,1,0:T(8,128)(2,1)S(1)}, u32[]{:S(2)}, u32[]{:S(2)}) collective-permute-start(bf16[4,96,256]{2,1,0:T(8,128)(2,1)S(1)} %get-tuple-element.31), channel_id=1, source_target_pairs={{0,9},{1,10},{2,11},{3,12},{4,13},{5,14},{6,15},{8,17},{9,18},{10,... | collective-permute-start | bytes 589832 | tf_op jit(solution)/shard_map/ppermute | solution.py:277
  11.2 7.5 %copy-start = (bf16[3,3,3,96,96]{4,3,2,1,0:T(8,128)(2,1)S(1)}, bf16[3,3,3,96,96]{4,3,2,1,0:T(8,128)(2,1)}, u32[]{:S(2)}) copy-start(bf16[3,3,3,96,96]{4,3,2,1,0:T(8,128)(2,1)} %weight_ref.1) | copy-start | bytes 1492996
  13.0 6.3 %collective-permute-start.2 = (bf16[4,96,256]{2,1,0:T(8,128)(2,1)S(1)}, bf16[4,96,256]{2,1,0:T(8,128)(2,1)S(1)}, u32[]{:S(2)}, u32[]{:S(2)}) collective-permute-start(bf16[4,96,256]{2,1,0:T(8,128)(2,1)S(1)} %get-tuple-element.30), channel_id=1, source_target_pairs={{0,8},{8,16},{16,24},{1,9},{9,17},{17,25},{2,10},{10,18},{18,26},{... | collective-permute-start | bytes 589832 | tf_op jit(solution)/shard_map/ppermute | solution.py:271
  16.8 4.9 %collective-permute-start = (bf16[4,96,384]{2,1,0:T(8,128)(2,1)S(1)}, bf16[4,96,384]{2,1,0:T(8,128)(2,1)S(1)}, u32[]{:S(2)}, u32[]{:S(2)}) collective-permute-start(bf16[4,96,384]{2,1,0:T(8,128)(2,1)S(1)} %get-tuple-element.26.mine_ref), channel_id=1, source_target_pairs={{0,8},{8,16},{16,24},{1,9},{9,17},{17,25},{2,10},{10,18},{18,26},{... | collective-permute-start | bytes 884744 | tf_op jit(solution)/shard_map/ppermute | solution.py:271
  19.3 2.5 %copy-start.1 = (bf16[96,192]{1,0:T(8,128)(2,1)S(1)}, bf16[96,192]{1,0:T(8,128)(2,1)}, u32[]{:S(2)}) copy-start(bf16[96,192]{1,0:T(8,128)(2,1)} %skip_ref.1) | copy-start | bytes 110596
  19.3 2.5 %copy-start.2 = (f32[96]{0:T(128)S(1)}, f32[96]{0:T(128)}, u32[]{:S(2)}) copy-start(f32[96]{0:T(128)} %param.17) | copy-start | bytes 1156
  19.3 2.5 %copy-start.3 = (f32[96]{0:T(128)S(1)}, f32[96]{0:T(128)}, u32[]{:S(2)}) copy-start(f32[96]{0:T(128)} %param.19) | copy-start | bytes 1156
  20.5 8.8 %collective-permute-start.4 = (bf16[4,96,256]{2,1,0:T(8,128)(2,1)S(1)}, bf16[4,96,256]{2,1,0:T(8,128)(2,1)S(1)}, u32[]{:S(2)}, u32[]{:S(2)}) collective-permute-start(bf16[4,96,256]{2,1,0:T(8,128)(2,1)S(1)} %get-tuple-element.34), channel_id=1, source_target_pairs={{1,0},{2,1},{3,2},{4,3},{5,4},{6,5},{7,6},{9,8},{10,9},{11,10},{12... | collective-permute-start | bytes 589832 | tf_op jit(solution)/shard_map/ppermute | solution.py:271
where the time goes:
time: 30.4 us; the launch traced here: 30.2 us
  starting transfers between devices  14.5 us (48%)
  Pallas kernels  9.75 us (32%)
  waiting for transfers between devices  5.72 us (19%)
    ppermute x4, starting transfers between devices, moved_by(): lax.ppermute(block, axis, [(i, i + distance) for i in devices if i + dist...  11.9 us
    pallas_call x6, Pallas kernels, call(): pl.pallas_call(kernel, out_shape=shapes[0] if single else tuple(shapes),...  9.75 us
    ppermute x4, waiting for transfers between devices, moved_by(): lax.ppermute(block, axis, [(i, i + distance) for i in devices if i + dist...  5.72 us
    ppermute x1, starting transfers between devices, moved_across(): return lax.ppermute(block, ('tm', 'rows'), route)  2.59 us
  transfers between devices with their start and end apart: 5, of which 1 were waited for; matrix products, arithmetic and copies ran while one was open for 0% of the time, Pallas kernels for 17%

commit v1 on v0

--- a/solution.py
+++ b/solution.py
@@ -242,16 +242,21 @@
             total_ref[out, :, cols] = total
 
 
-def last_kernel(total_ref, below_ref, out_ref):
+def last_kernel(total_ref, below_ref, out_hbm, out_ref, sems):
     frames, outs, height, width = out_ref.shape
+    copies = []
     for f in range(frames):
         rows = [total_ref[f, :, r * width : (r + 1) * width] for r in range(height)]
         for n in range(2):
             rows[height - 2 + n] = rows[height - 2 + n] + below_ref[f, :, n * width : (n + 1) * width].astype(F32)
         out_ref[f] = jnp.concatenate(rows, axis=1).reshape(outs, height, width).astype(BF16)
-
-
-def call(kernel, shapes, operands, flops, places=(), scratch=()):
+        copies.append(pltpu.make_async_copy(out_ref.at[f], out_hbm.at[f], sems.at[f]))
+        copies[f].start()
+    for copy in copies:
+        copy.wait()
+
+
+def call(kernel, shapes, operands, flops, places=(), scratch=(), result=VMEM):
     moved = sum(x.size * x.dtype.itemsize for x in operands) + sum(s.size * s.dtype.itemsize for s in shapes)
     single = len(shapes) == 1
     places = list(places) + [VMEM] * (len(operands) - len(places))
@@ -259,7 +264,7 @@
         kernel,
         out_shape=shapes[0] if single else tuple(shapes),
         in_specs=places,
-        out_specs=VMEM if single else tuple(VMEM for _ in shapes),
+        out_specs=result if single else tuple(VMEM for _ in shapes),
         scratch_shapes=list(scratch),
         cost_estimate=pl.CostEstimate(flops=flops, bytes_accessed=moved, transcendentals=0),
         compiler_params=pltpu.CompilerParams(vmem_limit_bytes=20 << 20),
@@ -342,7 +347,14 @@
         work * (height - 1) // 2,
         scratch=[pltpu.VMEM(((frames + 2) * deep_mid, (height - 1) * width), BF16)],
     )
-    return call(last_kernel, [shape((frames, outs, height, width), BF16)], (total, below), 1000)
+    return call(
+        last_kernel,
+        [shape((frames, outs, height, width), BF16)],
+        (total, below),
+        1000,
+        scratch=[pltpu.VMEM((frames, outs, height, width), BF16), pltpu.SemaphoreType.DMA((frames,))],
+        result=HBM,
+    )
 
 
 def solution(mesh):

time: 30.4 us -> 30.4 us (level)
  no operation moved by 1% of the time
where the time goes in v1:
time: 30.4 us; the launch traced here: 30.1 us
  starting transfers between devices  14.5 us (48%)
  Pallas kernels  9.68 us (32%)
  waiting for transfers between devices  5.72 us (19%)
    ppermute x4, starting transfers between devices, moved_by(): lax.ppermute(block, axis, [(i, i + distance) for i in devices if i + dist...  11.9 us
    pallas_call x6, Pallas kernels, call(): pl.pallas_call(kernel, out_shape=shapes[0] if single else tuple(shapes),...  9.68 us
    ppermute x4, waiting for transfers between devices, moved_by(): lax.ppermute(block, axis, [(i, i + distance) for i in devices if i + dist...  5.72 us
    ppermute x1, starting transfers between devices, moved_across(): return lax.ppermute(block, ('tm', 'rows'), route)  2.59 us
  transfers between devices with their start and end apart: 5, of which 1 were waited for; matrix products, arithmetic and copies ran while one was open for 0% of the time, Pallas kernels for 17%

profile of v1, /device:TPU:0, one launch (start us, length us, event | category | flops | bytes accessed | tf_op | source)
XLA Modules:
  0.0 30.1 jit_solution(16160100199593424226)
XLA Ops:
  0.0 0.0 copy-start.4
  0.0 0.0 copy-start.5
  0.0 0.0 copy-start.6
  0.0 3.7 %shard_map.100 = (bf16[288,1728]{1,0:T(8,128)(2,1)S(1)}, bf16[4,96,256]{2,1,0:T(8,128)(2,1)S(1)}, bf16[4,96,256]{2,1,0:T(8,128)(2,1)S(1)}, f32[6,96,384]{2,1,0:T...) custom-call(s32[16]{0:T(128)} %clip_hbm.1, bf16[4,192,4,128]{3,2,1,0:T(4,128)(2,1)} %lat_hbm.1, ...), custom_call_target="tpu_custom_call" | custom-call | flops 1019215872 | bytes 4891456 | tf_op jit(solution)/shard_map/pallas_call | solution.py:263
  3.7 4.9 %collective-permute-start.1 = (bf16[4,96,256]{2,1,0:T(8,128)(2,1)S(1)}, bf16[4,96,256]{2,1,0:T(8,128)(2,1)S(1)}, u32[]{:S(2)}, u32[]{:S(2)}) collective-permute-start(bf16[4,96,256]{2,1,0:T(8,128)(2,1)S(1)} %get-tuple-element.29), channel_id=1, source_target_pairs={{0,1},{1,2},{2,3},{3,4},{4,5},{5,6},{6,7},{8,9},{9,10},{10,11},{11... | collective-permute-start | bytes 589832 | tf_op jit(solution)/shard_map/ppermute | solution.py:276
  8.6 2.6 %collective-permute-start.3 = (bf16[4,96,256]{2,1,0:T(8,128)(2,1)S(1)}, bf16[4,96,256]{2,1,0:T(8,128)(2,1)S(1)}, u32[]{:S(2)}, u32[]{:S(2)}) collective-permute-start(bf16[4,96,256]{2,1,0:T(8,128)(2,1)S(1)} %get-tuple-element.31), channel_id=1, source_target_pairs={{0,9},{1,10},{2,11},{3,12},{4,13},{5,14},{6,15},{8,17},{9,18},{10,... | collective-permute-start | bytes 589832 | tf_op jit(solution)/shard_map/ppermute | solution.py:282
  11.2 0.0 copy-done.4
  11.2 0.0 copy-done.5
  11.2 0.0 copy-done.6
  11.2 0.0 copy-start
  11.2 1.8 %shard_map.101 = (f32[2,96,256]{2,1,0:T(8,128)S(1)}, bf16[4,96,256]{2,1,0:T(8,128)(2,1)S(1)}, bf16[4,96,384]{2,1,0:T(8,128)(2,1)S(1)}, bf16[2304,256]{1,0:T(8,128)(2,1)S(1)}, f32[2,96,128]{2,1,0:T(8,128)S(1)}) custom-call(bf16[12,16,128]{2,1,0:T(8,128)(2,1)S(1)} %get-tuple-element.20.keep_ref, bf16[4,192,4,128]{3,2,1,0:T(4,128)(2,1)S(1)} %get-tuple-element.21.lat_ref, ...), custom_call_target="tpu_custom_call" | custom-call | flops 1019215872 | bytes 4683264 | tf_op jit(solution)/shard_map/pallas_call | solution.py:263
  13.0 3.8 %collective-permute-start.2 = (bf16[4,96,256]{2,1,0:T(8,128)(2,1)S(1)}, bf16[4,96,256]{2,1,0:T(8,128)(2,1)S(1)}, u32[]{:S(2)}, u32[]{:S(2)}) collective-permute-start(bf16[4,96,256]{2,1,0:T(8,128)(2,1)S(1)} %get-tuple-element.30), channel_id=1, source_target_pairs={{0,8},{8,16},{16,24},{1,9},{9,17},{17,25},{2,10},{10,18},{18,26},{... | collective-permute-start | bytes 589832 | tf_op jit(solution)/shard_map/ppermute | solution.py:276
  16.8 1.9 %collective-permute-start = (bf16[4,96,384]{2,1,0:T(8,128)(2,1)S(1)}, bf16[4,96,384]{2,1,0:T(8,128)(2,1)S(1)}, u32[]{:S(2)}, u32[]{:S(2)}) collective-permute-start(bf16[4,96,384]{2,1,0:T(8,128)(2,1)S(1)} %get-tuple-element.26.mine_ref), channel_id=1, source_target_pairs={{0,8},{8,16},{16,24},{1,9},{9,17},{17,25},{2,10},{10,18},{18,26},{... | collective-permute-start | bytes 884744 | tf_op jit(solution)/shard_map/ppermute | solution.py:276
  18.8 0.0 copy-done
  18.8 0.5 %shard_map.102 = (f32[2,96,640]{2,1,0:T(8,128)S(1)}, bf16[288,864]{1,0:T(8,128)(2,1)S(1)}) custom-call(bf16[12,16,128]{2,1,0:T(8,128)(2,1)S(1)} %get-tuple-element.20.keep_ref, bf16[2304,256]{1,0:T(8,128)(2,1)S(1)} %get-tuple-element.24.xs_ref, bf16[288,1728]{1,0:T(8,128)(2,1)S(1)} %get-tuple-element.22.wt_ref, ...), custom_call_target="tpu_custom_call" | custom-call | flops 509607936 | bytes 4595712 | tf_op jit(solution)/shard_map/pallas_call | solution.py:263
  19.3 0.0 copy-start.1
  19.3 0.0 copy-start.2
  19.3 0.0 copy-start.3
  19.3 0.0 collective-permute-done.1.got_ref
  19.3 0.0 collective-permute-done.3.cross_ref
  19.3 0.0 collective-permute-done.2.before_ref
  19.3 1.1 %shard_map.103 = (bf16[4,96,256]{2,1,0:T(8,128)(2,1)S(1)}, f32[4,96,256]{2,1,0:T(8,128)S(1)}) custom-call(bf16[12,16,128]{2,1,0:T(8,128)(2,1)S(1)} %get-tuple-element.20.keep_ref, f32[2,96,640]{2,1,0:T(8,128)S(1)} %get-tuple-element.25.head_ref, f32[2,96,256]{2,1,0:T(8,128)S(1)} %get-tuple-element.28.part_ref, ...), custom_call_target="tpu_custom_call" | custom-call | flops 509607936 | bytes 2512896 | tf_op jit(solution)/shard_map/pallas_call | solution.py:263
  20.5 1.3 %collective-permute-start.4 = (bf16[4,96,256]{2,1,0:T(8,128)(2,1)S(1)}, bf16[4,96,256]{2,1,0:T(8,128)(2,1)S(1)}, u32[]{:S(2)}, u32[]{:S(2)}) collective-permute-start(bf16[4,96,256]{2,1,0:T(8,128)(2,1)S(1)} %get-tuple-element.34), channel_id=1, source_target_pairs={{1,0},{2,1},{3,2},{4,3},{5,4},{6,5},{7,6},{9,8},{10,9},{11,10},{12... | collective-permute-start | bytes 589832 | tf_op jit(solution)/shard_map/ppermute | solution.py:276
  21.8 0.0 collective-permute-done.before_ref
  21.8 0.0 copy-done.1
  21.8 0.0 copy-done.2
  21.8 0.0 copy-done.3
  21.8 1.7 %shard_map.104.total_ref = f32[4,96,512]{2,1,0:T(8,128)S(1)} custom-call(bf16[12,16,128]{2,1,0:T(8,128)(2,1)S(1)} %get-tuple-element.20.keep_ref, f32[2,96,640]{2,1,0:T(8,128)S(1)} %get-tuple-element.25.head_ref, bf16[4,96,384]{2,1,0:T(8,128)(2,1)S(1)} %get-tuple-element.26.mine_ref, bf16[4,96,384]{2,1,0:T(8,128)(2,1)S(1)} %collective-permute-done.before_ref, ...), custom_call_target="tpu_custom_call" | custom-call | flops 764411904 | bytes 3730176 | tf_op jit(solution)/shard_map/pallas_call | solution.py:263
  23.5 5.7 %collective-permute-done.4.below_ref = bf16[4,96,256]{2,1,0:T(8,128)(2,1)S(1)} collective-permute-done((bf16[4,96,256]{2,1,0:T(8,128)(2,1)S(1)}, bf16[4,96,256]{2,1,0:T(8,128)(2,1)S(1)}, u32[]{:S(2)}, u32[]{:S(2)}) %collective-permute-start.4) | collective-permute-done | bytes 196640 | tf_op jit(solution)/shard_map/ppermute | solution.py:276
  29.3 0.9 %shard_map.105 = bf16[4,96,4,128]{3,2,1,0:T(4,128)(2,1)} custom-call(f32[4,96,512]{2,1,0:T(8,128)S(1)} %shard_map.104.total_ref, bf16[4,96,256]{2,1,0:T(8,128)(2,1)S(1)} %collective-permute-done.4.below_ref), custom_call_target="tpu_custom_call" | custom-call | flops 1000 | bytes 1376256 | tf_op jit(solution)/shard_map/pallas_call | solution.py:263
Async XLA Ops:
  0.0 11.2 %copy-start.4 = (f32[192]{0:T(256)S(1)}, f32[192]{0:T(256)}, u32[]{:S(2)}) copy-start(f32[192]{0:T(256)} %param.12) | copy-start | bytes 2308
  0.0 11.2 %copy-start.5 = (f32[96]{0:T(128)S(1)}, f32[96]{0:T(128)}, u32[]{:S(2)}) copy-start(f32[96]{0:T(128)} %param.14) | copy-start | bytes 1156
  0.0 11.2 %copy-start.6 = (f32[96]{0:T(128)S(1)}, f32[96]{0:T(128)}, u32[]{:S(2)}) copy-start(f32[96]{0:T(128)} %param.15) | copy-start | bytes 1156
  3.7 15.6 %collective-permute-start.1 = (bf16[4,96,256]{2,1,0:T(8,128)(2,1)S(1)}, bf16[4,96,256]{2,1,0:T(8,128)(2,1)S(1)}, u32[]{:S(2)}, u32[]{:S(2)}) collective-permute-start(bf16[4,96,256]{2,1,0:T(8,128)(2,1)S(1)} %get-tuple-element.29), channel_id=1, source_target_pairs={{0,1},{1,2},{2,3},{3,4},{4,5},{5,6},{6,7},{8,9},{9,10},{10,11},{11... | collective-permute-start | bytes 589832 | tf_op jit(solution)/shard_map/ppermute | solution.py:276
  8.6 10.7 %collective-permute-start.3 = (bf16[4,96,256]{2,1,0:T(8,128)(2,1)S(1)}, bf16[4,96,256]{2,1,0:T(8,128)(2,1)S(1)}, u32[]{:S(2)}, u32[]{:S(2)}) collective-permute-start(bf16[4,96,256]{2,1,0:T(8,128)(2,1)S(1)} %get-tuple-element.31), channel_id=1, source_target_pairs={{0,9},{1,10},{2,11},{3,12},{4,13},{5,14},{6,15},{8,17},{9,18},{10,... | collective-permute-start | bytes 589832 | tf_op jit(solution)/shard_map/ppermute | solution.py:282
  11.2 7.5 %copy-start = (bf16[3,3,3,96,96]{4,3,2,1,0:T(8,128)(2,1)S(1)}, bf16[3,3,3,96,96]{4,3,2,1,0:T(8,128)(2,1)}, u32[]{:S(2)}) copy-start(bf16[3,3,3,96,96]{4,3,2,1,0:T(8,128)(2,1)} %weight_ref.1) | copy-start | bytes 1492996
  13.0 6.3 %collective-permute-start.2 = (bf16[4,96,256]{2,1,0:T(8,128)(2,1)S(1)}, bf16[4,96,256]{2,1,0:T(8,128)(2,1)S(1)}, u32[]{:S(2)}, u32[]{:S(2)}) collective-permute-start(bf16[4,96,256]{2,1,0:T(8,128)(2,1)S(1)} %get-tuple-element.30), channel_id=1, source_target_pairs={{0,8},{8,16},{16,24},{1,9},{9,17},{17,25},{2,10},{10,18},{18,26},{... | collective-permute-start | bytes 589832 | tf_op jit(solution)/shard_map/ppermute | solution.py:276
  16.8 4.9 %collective-permute-start = (bf16[4,96,384]{2,1,0:T(8,128)(2,1)S(1)}, bf16[4,96,384]{2,1,0:T(8,128)(2,1)S(1)}, u32[]{:S(2)}, u32[]{:S(2)}) collective-permute-start(bf16[4,96,384]{2,1,0:T(8,128)(2,1)S(1)} %get-tuple-element.26.mine_ref), channel_id=1, source_target_pairs={{0,8},{8,16},{16,24},{1,9},{9,17},{17,25},{2,10},{10,18},{18,26},{... | collective-permute-start | bytes 884744 | tf_op jit(solution)/shard_map/ppermute | solution.py:276
  19.3 2.5 %copy-start.1 = (bf16[96,192]{1,0:T(8,128)(2,1)S(1)}, bf16[96,192]{1,0:T(8,128)(2,1)}, u32[]{:S(2)}) copy-start(bf16[96,192]{1,0:T(8,128)(2,1)} %skip_ref.1) | copy-start | bytes 110596
  19.3 2.5 %copy-start.2 = (f32[96]{0:T(128)S(1)}, f32[96]{0:T(128)}, u32[]{:S(2)}) copy-start(f32[96]{0:T(128)} %param.17) | copy-start | bytes 1156
  19.3 2.5 %copy-start.3 = (f32[96]{0:T(128)S(1)}, f32[96]{0:T(128)}, u32[]{:S(2)}) copy-start(f32[96]{0:T(128)} %param.19) | copy-start | bytes 1156
  20.5 8.8 %collective-permute-start.4 = (bf16[4,96,256]{2,1,0:T(8,128)(2,1)S(1)}, bf16[4,96,256]{2,1,0:T(8,128)(2,1)S(1)}, u32[]{:S(2)}, u32[]{:S(2)}) collective-permute-start(bf16[4,96,256]{2,1,0:T(8,128)(2,1)S(1)} %get-tuple-element.34), channel_id=1, source_target_pairs={{1,0},{2,1},{3,2},{4,3},{5,4},{6,5},{7,6},{9,8},{10,9},{11,10},{12... | collective-permute-start | bytes 589832 | tf_op jit(solution)/shard_map/ppermute | solution.py:276
